TPU v7x, 128 devices: a whole 4x4x4 slice. The times are simulated.
128 devices in a mesh: row: 8 (over x, core), col: 16 (over y, z).
Axes of the slice: x: 4, y: 4, z: 4, core: 2. Of those that a mesh axis runs over, the one named last changes fastest.
Arguments:
- parent_front: float32 [16384, 16384], P('row', 'col'), as said below
- child_panels: float32 [8, 4096, 512], P('row', 'col'), may hold values from -6 to 6
- child_inverses: float32 [8, 512, 512], P('row'), as said below
- parent_index: int32 [8, 16], replicated, may hold values from 2 to 63, as said below
Outputs:
- panel: float32 [16384, 512], P('row')
- schur: float32 [16384, 16384], P('row', 'col')
Inputs may be any that keep to these rules, and one draw needn't show every extreme that they name: `parent_index`: entry (g, u) names the parent tile that receives tile row and tile column u of child g's update. Seen in blocks of 4 consecutive tiles, each child names every block exactly once, and at a given u the children name different blocks. No entry names one of the first 2 tiles. `parent_front`: Symmetric. In its leading 2 * 256 rows and columns, each diagonal entry is positive and exceeds the sum of magnitudes of the other entries of its row within that block. `child_inverses`: each matrix is lower triangular with a positive diagonal.
All inputs are finite; a program needn't handle non-finite values.
Results may differ from a plain program's by a relative error of at most 0.0003.
Values sent between devices are 32-bit elements; how exact they have to be, the bound alone decides.
A program may use at most 128 MiB of HBM per device.

v0:
```python
import jax
import jax.numpy as jnp
from jax import lax
from jax.sharding import PartitionSpec as P

TILE = 256
PCT = 4
NSP = 2


def from_root(block, axis, holder):
    block = jnp.where(lax.axis_index(axis) == holder, block, jnp.zeros_like(block))
    return lax.psum(block, axis)


def product(matrix_a, matrix_b):
    return jnp.dot(
        matrix_a, matrix_b, precision=lax.Precision.HIGHEST, preferred_element_type=jnp.float32
    )


def product_rows(matrix_a, matrix_b):
    return lax.dot_general(
        matrix_a,
        matrix_b,
        (((1,), (1,)), ((), ())),
        precision=lax.Precision.HIGHEST,
        preferred_element_type=jnp.float32,
    )


def place_tiles(received, row_tiles, col_tiles, live_mask, tile_count):
    target = row_tiles * PCT + col_tiles
    onehot = (target[None, :] == jnp.arange(tile_count)[:, None]).astype(jnp.float32) * live_mask[
        None, :
    ]
    flat_tiles = received.reshape(received.shape[0], TILE * TILE)
    return product(onehot, flat_tiles)


def per_device(parent_front, child_panels, child_inverses, parent_index):
    row_devices = lax.axis_size("row")
    col_devices = lax.axis_size("col")
    here_row = lax.axis_index("row")
    here_col = lax.axis_index("col")
    per_block = col_devices // row_devices
    row_count = PCT * per_block
    tile_count = row_count * PCT
    own_factor = product_rows(child_panels[0], child_inverses[0])
    my_list = lax.dynamic_index_in_dim(parent_index, here_row, 0, keepdims=False)
    block_of = parent_index // PCT
    update_col = product_rows(lax.all_gather(own_factor, "col", axis=0, tiled=True), own_factor)
    dest_row = my_list // PCT // per_block
    tile_ids = jnp.arange(col_devices, dtype=jnp.int32)
    same_dest = (dest_row[None, :] == dest_row[:, None]) & (tile_ids[None, :] < tile_ids[:, None])
    slot_index = jnp.sum(same_dest.astype(jnp.int32), axis=1)
    position = dest_row * per_block + slot_index
    send_order = jnp.zeros((col_devices,), jnp.int32).at[position].set(tile_ids)
    outgoing = update_col.reshape(col_devices, TILE, TILE)[send_order].reshape(
        row_devices, per_block, TILE, TILE
    )
    arrived = lax.all_to_all(outgoing, "row", split_axis=0, concat_axis=0, tiled=True)
    local_mask = block_of // per_block == here_row
    slot_rank = jnp.cumsum(local_mask.astype(jnp.int32), axis=1) - 1
    slot_ids = jnp.arange(per_block, dtype=jnp.int32)
    slot_pick = (
        local_mask[:, :, None] & (slot_rank[:, :, None] == slot_ids[None, None, :])
    ).astype(jnp.int32)
    row_tile = jnp.sum(parent_index[:, :, None] * slot_pick, axis=1) - here_row * row_count
    sent_to = lax.dynamic_index_in_dim(block_of, here_col, 1, keepdims=False)
    col_route = (sent_to[None, :] == jnp.arange(col_devices)[:, None]).astype(jnp.float32)
    outgoing_cols = product(col_route, arrived.reshape(row_devices, -1)).reshape(
        col_devices, per_block, TILE, TILE
    )
    arrived_cols = lax.all_to_all(outgoing_cols, "col", split_axis=0, concat_axis=0, tiled=True)
    col_match = (block_of == here_col).astype(jnp.int32)
    col_tile = parent_index - here_col * PCT
    rows_from = jnp.sum(row_tile[:, None, :] * col_match[:, :, None], axis=0)
    cols_from = jnp.sum(col_tile * col_match, axis=0)
    live_from = jnp.sum(col_match, axis=0).astype(jnp.float32)
    cols_flat = (cols_from[:, None] + jnp.zeros_like(rows_from)).reshape(-1)
    live_flat = (live_from[:, None] + jnp.zeros(rows_from.shape, jnp.float32)).reshape(-1)
    contrib = place_tiles(
        arrived_cols.reshape(-1, TILE, TILE),
        rows_from.reshape(-1),
        cols_flat,
        live_flat,
        tile_count,
    )
    contrib = (
        contrib.reshape(row_count, PCT, TILE, TILE)
        .transpose(0, 2, 1, 3)
        .reshape(row_count * TILE, PCT * TILE)
    )
    work_matrix = parent_front - contrib
    identity = jnp.eye(TILE, dtype=jnp.float32)
    owner = (here_row == 0) & (here_col == 0)
    row_tile_index = here_row * row_count + jnp.arange(row_count * TILE) // TILE
    columns = []
    for step in range(NSP):
        offset = step * TILE
        diag_tile = jnp.where(
            owner, work_matrix[offset : offset + TILE, offset : offset + TILE], identity
        )
        pivot_tile = jnp.linalg.cholesky(diag_tile)
        inverse = lax.linalg.triangular_solve(pivot_tile, identity, left_side=True, lower=True)
        pivot_pair = from_root(jnp.stack([pivot_tile, inverse]), "row", 0)
        pivot_tile = pivot_pair[0]
        inverse = pivot_pair[1]
        factored = product_rows(work_matrix[:, offset : offset + TILE], inverse)
        factored = jnp.where(row_tile_index[:, None] < step, jnp.zeros_like(factored), factored)
        current = factored[offset : offset + TILE]
        rows_panel, inverse = (
            from_root(
                factored.at[offset : offset + TILE].set(
                    jnp.where(here_row == 0, pivot_tile, current)
                ),
                "col",
                0,
            ),
            from_root(inverse, "col", 0),
        )
        source = from_root(rows_panel, "row", here_col // per_block)
        col_panel = lax.dynamic_slice_in_dim(
            source, here_col % per_block * PCT * TILE, PCT * TILE, 0
        )
        work_matrix = work_matrix - product_rows(rows_panel, col_panel)
        columns.append(rows_panel)
    return (jnp.concatenate(columns, axis=1), work_matrix)


def solution(mesh):
    placed = (P("row", "col"), P("row", "col", None), P("row", None, None), P())
    return jax.shard_map(
        per_device,
        mesh=mesh,
        in_specs=placed,
        out_specs=(P("row", None), P("row", "col")),
        check_vma=False,
    )
```

profile of v0, /device:TPU:0, one launch (start us, length us, event | category | flops | bytes accessed | tf_op | source)
XLA Modules:
  0.0 993.7 jit_solution(9929762409883196764)
XLA Ops:
  14.3 70.5 %all-gather.2.cloned.1.call-done = f32[4096,512]{1,0:T(8,128)} async-done(((f32[256,512]{1,0:T(8,128)}), f32[4096,512]{1,0:T(8,128)}) %all-gather.2.cloned.1.call-update) | async-done | bytes 8388624 | tf_op jit(solution)/shard_map/all_gather | solution.py:52
  84.8 10.6 %fusion.69 = f32[4096,256]{1,0:T(8,128)} fusion(f32[4096,512]{1,0:T(8,128)} %all-gather.2.cloned.1.call-done, f32[256,512]{1,0:T(8,128)} %fusion.5), kind=kOutput, calls=%fused_computation.186 | convolution fusion | flops 6442450944 | bytes 13107200 | tf_op jit(solution)/shard_map/dot_general | solution.py:23
  105.5 49.4 %all-to-all-done = f32[8,2,256,256]{3,2,1,0:T(8,128)} async-done(((f32[8,2,256,256]{3,2,1,0:T(8,128)}), f32[8,2,256,256]{3,2,1,0:T(8,128)}, u32[]{:S(2)}, u32[]{:S(2)}) %all-to-all-start) | async-done | bytes 4194336 | tf_op jit(solution)/shard_map/all_to_all | solution.py:62
  186.9 134.8 %all-to-all-done.1 = f32[16,2,256,256]{3,2,1,0:T(8,128)} async-done(((f32[16,2,256,256]{3,2,1,0:T(8,128)}), f32[16,2,256,256]{3,2,1,0:T(8,128)}, u32[]{:S(2)}, u32[]{:S(2)}) %all-to-all-start.1) | async-done | bytes 8388640 | tf_op jit(solution)/shard_map/all_to_all | solution.py:75
  321.7 17.3 %fusion.2 = f32[8,256,4,256]{3,0,1,2:T(8,128)} fusion(f32[32]{0:T(128)S(1)} %mul.78, s32[8,4]{0,1:T(4,128)S(1)} %multiply_add_fusion, s32[32]{0:T(128)S(1)} %add.154, f32[4,8,256,256]{3,2,1,0:T(8,128)} %bitcast.51), kind=kOutput, calls=%fused_computation.12 | convolution fusion | flops 805308416 | bytes 16777600 | tf_op jit(solution)/shard_map/dot_general | solution.py:17
  339.0 10.8 %copy.36 = f32[8,256,4,256]{1,0,3,2:T(8,128)} copy(f32[8,256,4,256]{3,0,1,2:T(8,128)} %fusion.2) | data formatting | bytes 16777216 | tf_op jit(solution)/shard_map/transpose | solution.py:92
  349.8 10.7 %copy.54 = f32[128,8,8,256]{3,1,2,0:T(8,128)} copy(f32[128,8,8,256]{3,2,1,0:T(8,128)} %bitcast.170) | data formatting | bytes 16777216
  360.5 11.9 %sub.79 = f32[2048,1024]{0,1:T(8,128)} subtract(f32[2048,1024]{0,1:T(8,128)} %copy.37, f32[2048,1024]{0,1:T(8,128)} %bitcast.169) | non-fusion elementwise | flops 2097152 | bytes 25165824 | tf_op jit(solution)/shard_map/sub | solution.py:95
  374.5 11.7 %cholesky.130 = f32[128,128]{1,0:T(8,128)S(1)} custom-call(f32[128,128]{1,0:T(8,128)S(1)} %cholesky.194), custom_call_target="Cholesky" | custom-call | tf_op jit(solution)/shard_map/jit(cholesky)/cholesky | solution.py:105
  386.3 10.0 %custom-call.13 = f32[1,128,128]{1,2,0:T(8,128)S(1)} custom-call(f32[1,128,128]{2,1,0:T(8,128)S(1)} %get-tuple-element.90), custom_call_target="InvertDiagBlocksLowerTriangular" | custom-call | tf_op jit(solution)/shard_map/jit(cholesky)/cholesky | solution.py:105
  396.7 11.7 %cholesky.147 = f32[128,128]{1,0:T(8,128)S(1)} custom-call(f32[128,128]{1,0:T(8,128)S(1)} %convolution_subtract_fusion.5), custom_call_target="Cholesky" | custom-call | tf_op jit(solution)/shard_map/jit(cholesky)/cholesky | solution.py:105
  414.7 19.7 %custom-call.14 = f32[2,128,128]{1,2,0:T(8,128)S(1)} custom-call(f32[2,128,128]{2,1,0:T(8,128)S(1)} %get-tuple-element.42), custom_call_target="InvertDiagBlocksLowerTriangular" | custom-call | tf_op jit(solution)/shard_map/triangular_solve/custom-call.0 | solution.py:106
  436.3 63.0 %all-reduce.8.cloned.1.call-done = f32[2,256,256]{2,1,0:T(8,128)} async-done(((f32[2,256,256]{2,1,0:T(8,128)}), f32[2,256,256]{2,1,0:T(8,128)}) %all-reduce.8.cloned.1.call-update) | async-done | bytes 524304 | tf_op jit(solution)/shard_map/psum | solution.py:13
  506.1 89.7 %all-reduce.10.cloned.1.call-done = f32[2048,256]{1,0:T(8,128)} async-done(((f32[2048,256]{1,0:T(8,128)}), f32[2048,256]{1,0:T(8,128)}) %all-reduce.10.cloned.1.call-update) | async-done | bytes 2097168 | tf_op jit(solution)/shard_map/psum | solution.py:13
  599.1 64.4 %all-reduce.12.cloned.1.call-done = f32[2048,256]{1,0:T(8,128)} async-done(((f32[2048,256]{1,0:T(8,128)}), f32[2048,256]{1,0:T(8,128)}) %all-reduce.12.cloned.1.call-update) | async-done | bytes 2097168 | tf_op jit(solution)/shard_map/psum | solution.py:13
  663.6 10.5 %convolution_subtract_fusion.1 = f32[2048,1024]{0,1:T(8,128)S(1)} fusion(f32[2048,1024]{0,1:T(8,128)} %sub.79, f32[2048,256]{1,0:T(8,128)S(1)} %copy-done.3, f32[2048,256]{1,0:T(8,128)} %all-reduce.12.cloned.1.call-done, s32[]{:T(128)S(6)} %select_n.189), kind=kOutput, calls=%fused_computation.10 | convolution fusion | flops 6444548096 | bytes 19922948 | tf_op jit(solution)/shard_map/dot_general | solution.py:23
  678.6 11.7 %cholesky.164 = f32[128,128]{1,0:T(8,128)S(1)} custom-call(f32[128,128]{1,0:T(8,128)S(1)} %cholesky.197), custom_call_target="Cholesky" | custom-call | tf_op jit(solution)/shard_map/jit(cholesky)/cholesky | solution.py:105
  691.0 9.8 custom-call.15
  701.3 11.7 %cholesky.181 = f32[128,128]{1,0:T(8,128)S(1)} custom-call(f32[128,128]{1,0:T(8,128)S(1)} %convolution_subtract_fusion.4), custom_call_target="Cholesky" | custom-call | tf_op jit(solution)/shard_map/jit(cholesky)/cholesky | solution.py:105
  719.3 19.9 %custom-call.16 = f32[2,128,128]{1,2,0:T(8,128)S(1)} custom-call(f32[2,128,128]{2,1,0:T(8,128)S(1)} %get-tuple-element.43), custom_call_target="InvertDiagBlocksLowerTriangular" | custom-call | tf_op jit(solution)/shard_map/triangular_solve/custom-call.0 | solution.py:106
  741.2 60.2 %all-reduce.14.cloned.1.call-done = f32[2,256,256]{2,1,0:T(8,128)} async-done(((f32[2,256,256]{2,1,0:T(8,128)}), f32[2,256,256]{2,1,0:T(8,128)}) %all-reduce.14.cloned.1.call-update) | async-done | bytes 524304 | tf_op jit(solution)/shard_map/psum | solution.py:13
  808.2 89.8 %all-reduce.16.cloned.1.call-done = f32[2048,256]{1,0:T(8,128)} async-done(((f32[2048,256]{1,0:T(8,128)}), f32[2048,256]{1,0:T(8,128)}) %all-reduce.16.cloned.1.call-update) | async-done | bytes 2097168 | tf_op jit(solution)/shard_map/psum | solution.py:13
  905.3 60.0 %all-reduce.18.cloned.1.call-done = f32[2048,256]{1,0:T(8,128)} async-done(((f32[2048,256]{1,0:T(8,128)}), f32[2048,256]{1,0:T(8,128)}) %all-reduce.18.cloned.1.call-update) | async-done | bytes 2097168 | tf_op jit(solution)/shard_map/psum | solution.py:13
  965.3 11.8 %convolution_subtract_fusion = f32[2048,1024]{0,1:T(8,128)} fusion(f32[2048,1024]{0,1:T(8,128)} %copy-done.2, f32[2048,256]{1,0:T(8,128)} %all-reduce.16.cloned.1.call-done, f32[2048,256]{1,0:T(8,128)} %all-reduce.18.cloned.1.call-done, s32[]{:T(128)S(6)} %select_n.189), kind=kOutput, calls=%fused_computation.9 | convolution fusion | flops 6444548096 | bytes 19922948 | tf_op jit(solution)/shard_map/dot_general | solution.py:23
  (124 shorter events, 112.5 us)
Async XLA Ops:
  7.2 1.2 copy-start
  7.2 77.6 %all-gather.2.cloned.1.call-start = ((), (), s32[]{:S(2)}) async-start(), calls=%async_computation.2 | async-start | bytes 8912896 | tf_op jit(solution)/shard_map/all_gather | solution.py:52
  100.4 4.9 copy-start.6
  100.4 54.5 %all-to-all-start = ((f32[8,2,256,256]{3,2,1,0:T(8,128)}), f32[8,2,256,256]{3,2,1,0:T(8,128)}, u32[]{:S(2)}, u32[]{:S(2)}) async-start(f32[8,2,256,256]{3,2,1,0:T(8,128)} %bitcast.172), calls=%async_computation | async-start | bytes 8388608 | tf_op jit(solution)/shard_map/all_to_all | solution.py:62
  171.3 150.4 %all-to-all-start.1 = ((f32[16,2,256,256]{3,2,1,0:T(8,128)}), f32[16,2,256,256]{3,2,1,0:T(8,128)}, u32[]{:S(2)}, u32[]{:S(2)}) async-start(f32[16,2,256,256]{3,2,1,0:T(8,128)} %copy.34), calls=%async_computation.1 | async-start | bytes 16777216 | tf_op jit(solution)/shard_map/all_to_all | solution.py:75
  176.7 322.7 %all-reduce.8.cloned.1.call-start = ((), (), s32[]{:S(2)}) async-start(), calls=%async_computation.3 | async-start | bytes 1048576 | tf_op jit(solution)/shard_map/psum | solution.py:13
  436.3 159.6 %all-reduce.10.cloned.1.call-start = ((), (), s32[]{:S(2)}) async-start(), calls=%async_computation.4 | async-start | bytes 4194304 | tf_op jit(solution)/shard_map/psum | solution.py:13
  499.3 5.2 copy-start.5
  506.0 157.5 %all-reduce.12.cloned.1.call-start = ((), (), s32[]{:S(2)}) async-start(), calls=%async_computation.5 | async-start | bytes 4194304 | tf_op jit(solution)/shard_map/psum | solution.py:13
  595.8 67.7 %copy-start.3 = (f32[2048,256]{1,0:T(8,128)S(1)}, f32[2048,256]{1,0:T(8,128)}, u32[]{:S(2)}) copy-start(f32[2048,256]{1,0:T(8,128)} %all-reduce.10.cloned.1.call-done) | copy-start | bytes 6291460
  599.1 202.4 %all-reduce.14.cloned.1.call-start = ((), (), s32[]{:S(2)}) async-start(), calls=%async_computation.6 | async-start | bytes 1048576 | tf_op jit(solution)/shard_map/psum | solution.py:13
  674.0 3.4 copy-start.2
  741.2 156.8 %all-reduce.16.cloned.1.call-start = ((), (), s32[]{:S(2)}) async-start(), calls=%async_computation.7 | async-start | bytes 4194304 | tf_op jit(solution)/shard_map/psum | solution.py:13
  801.5 5.2 copy-start.4
  808.2 157.1 %all-reduce.18.cloned.1.call-start = ((), (), s32[]{:S(2)}) async-start(), calls=%async_computation.8 | async-start | bytes 4194304 | tf_op jit(solution)/shard_map/psum | solution.py:13
  977.1 9.3 copy-start.1
Sparse Core Ops, SparseCore 0:
  11.4 73.3 all-gather.1
  436.4 62.9 all-reduce.7
  506.2 89.6 all-reduce.9
  599.2 64.3 all-reduce.11
  741.3 60.1 all-reduce.13
  808.3 89.6 all-reduce.15
  901.2 64.0 all-reduce.17
where the time goes:
time: 999 us; the launch traced here: 994 us
  waiting for transfers between devices  682 us (68%)
  other arithmetic  141 us (14%)
  local copies, waits for them, and re-layouts  71.9 us (7%)
  matrix products  70 us (7%)
  between operations  17.6 us (2%)
  starting transfers between devices  10.7 us (1%)
    psum x6, waiting for transfers between devices, from_root(): return lax.psum(block, axis)  427 us
    all_to_all x1, waiting for transfers between devices, per_device(): lax.all_to_all(outgoing_cols, 'col', split_axis=0, concat_axis=0, tiled=T...  135 us
    all_gather x1, waiting for transfers between devices, per_device(): lax.all_gather(own_factor, 'col', axis=0, tiled=True)  70.5 us
    another operation x13, other arithmetic, per_device(): pivot_tile = jnp.linalg.cholesky(diag_tile)  68.8 us
    all_to_all x1, waiting for transfers between devices, per_device(): lax.all_to_all(outgoing, 'row', split_axis=0, concat_axis=0, tiled=True)  49.4 us
    dot_general x6, matrix products, product_rows(): lax.dot_general(matrix_a, matrix_b, (((1,), (1,)), ((), ())), precision=l...  46 us
    another operation x3, other arithmetic, per_device(): lax.linalg.triangular_solve(pivot_tile, identity, left_side=True, lower=T...  39.6 us
    unnamed x18, local copies, waits for them, and re-layouts  38.4 us
  transfers between devices with their start and end apart: 9, of which 9 were waited for; matrix products, arithmetic and copies ran while one was open for 2% of the time, Pallas kernels for 0%

commit v1 on v0

--- a/solution.py
+++ b/solution.py
@@ -49,7 +49,12 @@
     own_factor = product_rows(child_panels[0], child_inverses[0])
     my_list = lax.dynamic_index_in_dim(parent_index, here_row, 0, keepdims=False)
     block_of = parent_index // PCT
-    update_col = product_rows(lax.all_gather(own_factor, "col", axis=0, tiled=True), own_factor)
+
+    def carry_patch(x0, shard_axis):
+        e_now = jnp.concatenate([x0 for _ in range(lax.psum(1, axis_name=shard_axis))], 0)
+        return lax.all_to_all(e_now, axis_name=shard_axis, split_axis=0, concat_axis=0, tiled=True)
+
+    update_col = product_rows(carry_patch(own_factor, "col"), own_factor)
     dest_row = my_list // PCT // per_block
     tile_ids = jnp.arange(col_devices, dtype=jnp.int32)
     same_dest = (dest_row[None, :] == dest_row[:, None]) & (tile_ids[None, :] < tile_ids[:, None])

time: 999 us -> 1090 us (1.091)
  waiting for transfers between devices: 682 us -> 758 us
  starting transfers between devices: 10.7 us -> 21.9 us
    all_to_all x0 -> x1, waiting for transfers between devices: none -> 147 us  [carry_patch(): lax.all_to_all(e_now, axis_name=shard_axis, split_axis=0, concat_axis=0,...]
    all_gather x1 -> x0, waiting for transfers between devices: 70.5 us -> none  [per_device(): lax.all_gather(own_factor, 'col', axis=0, tiled=True)]
    unnamed x18 -> x30, local copies, waits for them, and re-layouts: 38.4 us -> 42.2 us
  transfers between devices with their start and end apart: 9 -> 9, of which waited for: 9 -> 9; matrix products, arithmetic and copies ran while one was open for 2% -> 1% of each run, Pallas kernels for 0% -> 0%
where the time goes in v1:
time: 1090 us; the launch traced here: 1080 us
  waiting for transfers between devices  758 us (70%)
  other arithmetic  141 us (13%)
  local copies, waits for them, and re-layouts  75.8 us (7%)
  matrix products  69 us (6%)
  starting transfers between devices  21.9 us (2%)
  between operations  17.7 us (2%)
    psum x6, waiting for transfers between devices, from_root(): return lax.psum(block, axis)  427 us
    all_to_all x1, waiting for transfers between devices, carry_patch(): lax.all_to_all(e_now, axis_name=shard_axis, split_axis=0, concat_axis=0,...  147 us
    all_to_all x1, waiting for transfers between devices, per_device(): lax.all_to_all(outgoing_cols, 'col', split_axis=0, concat_axis=0, tiled=T...  135 us
    another operation x13, other arithmetic, per_device(): pivot_tile = jnp.linalg.cholesky(diag_tile)  68.8 us
    all_to_all x1, waiting for transfers between devices, per_device(): lax.all_to_all(outgoing, 'row', split_axis=0, concat_axis=0, tiled=True)  49.4 us
    dot_general x6, matrix products, product_rows(): lax.dot_general(matrix_a, matrix_b, (((1,), (1,)), ((), ())), precision=l...  45.1 us
    unnamed x30, local copies, waits for them, and re-layouts  42.2 us
    another operation x3, other arithmetic, per_device(): lax.linalg.triangular_solve(pivot_tile, identity, left_side=True, lower=T...  39.6 us
  transfers between devices with their start and end apart: 9, of which 9 were waited for; matrix products, arithmetic and copies ran while one was open for 1% of the time, Pallas kernels for 0%

profile of v1, /device:TPU:0, one launch (start us, length us, event | category | flops | bytes accessed | tf_op | source)
XLA Modules:
  0.0 1084.0 jit_solution(15797135929213506697)
XLA Ops:
  23.8 146.7 %all-to-all-done = f32[16,256,512]{2,1,0:T(8,128)} async-done(((f32[16,256,512]{2,1,0:T(8,128)}), f32[16,256,512]{2,1,0:T(8,128)}, u32[]{:S(2)}, u32[]{:S(2)}) %all-to-all-start) | async-done | bytes 8388640 | tf_op jit(solution)/shard_map/all_to_all | solution.py:55
  170.6 10.5 fusion.9
  191.0 49.4 %all-to-all-done.1 = f32[8,2,256,256]{3,2,1,0:T(8,128)} async-done(((f32[8,2,256,256]{3,2,1,0:T(8,128)}), f32[8,2,256,256]{3,2,1,0:T(8,128)}, u32[]{:S(2)}, u32[]{:S(2)}) %all-to-all-start.1) | async-done | bytes 4194336 | tf_op jit(solution)/shard_map/all_to_all | solution.py:67
  275.5 134.8 %all-to-all-done.2 = f32[16,2,256,256]{3,2,1,0:T(8,128)} async-done(((f32[16,2,256,256]{3,2,1,0:T(8,128)}), f32[16,2,256,256]{3,2,1,0:T(8,128)}, u32[]{:S(2)}, u32[]{:S(2)}) %all-to-all-start.2) | async-done | bytes 8388640 | tf_op jit(solution)/shard_map/all_to_all | solution.py:80
  410.3 17.3 %fusion.2 = f32[8,256,4,256]{3,0,1,2:T(8,128)} fusion(f32[32]{0:T(128)S(1)} %mul.78, s32[8,4]{0,1:T(4,128)S(1)} %multiply_add_fusion, s32[32]{0:T(128)S(1)} %add.154, f32[4,8,256,256]{3,2,1,0:T(8,128)} %bitcast.52), kind=kOutput, calls=%fused_computation.12 | convolution fusion | flops 805308416 | bytes 16777600 | tf_op jit(solution)/shard_map/dot_general | solution.py:17
  427.6 10.8 copy.36
  438.4 10.7 copy.54
  449.1 11.9 %sub.79 = f32[2048,1024]{0,1:T(8,128)} subtract(f32[2048,1024]{0,1:T(8,128)} %copy.37, f32[2048,1024]{0,1:T(8,128)} %bitcast.174) | non-fusion elementwise | flops 2097152 | bytes 25165824 | tf_op jit(solution)/shard_map/sub | solution.py:100
  463.1 11.7 %cholesky.130 = f32[128,128]{1,0:T(8,128)S(1)} custom-call(f32[128,128]{1,0:T(8,128)S(1)} %cholesky.194), custom_call_target="Cholesky" | custom-call | tf_op jit(solution)/shard_map/jit(cholesky)/cholesky | solution.py:110
  474.8 10.0 custom-call.13
  485.3 11.7 %cholesky.147 = f32[128,128]{1,0:T(8,128)S(1)} custom-call(f32[128,128]{1,0:T(8,128)S(1)} %convolution_subtract_fusion.5), custom_call_target="Cholesky" | custom-call | tf_op jit(solution)/shard_map/jit(cholesky)/cholesky | solution.py:110
  503.2 19.7 %custom-call.14 = f32[2,128,128]{1,2,0:T(8,128)S(1)} custom-call(f32[2,128,128]{2,1,0:T(8,128)S(1)} %get-tuple-element.42), custom_call_target="InvertDiagBlocksLowerTriangular" | custom-call | tf_op jit(solution)/shard_map/triangular_solve/custom-call.0 | solution.py:111
  524.9 63.0 %all-reduce.8.cloned.1.call-done = f32[2,256,256]{2,1,0:T(8,128)} async-done(((f32[2,256,256]{2,1,0:T(8,128)}), f32[2,256,256]{2,1,0:T(8,128)}) %all-reduce.8.cloned.1.call-update) | async-done | bytes 524304 | tf_op jit(solution)/shard_map/psum | solution.py:13
  595.5 89.7 %all-reduce.10.cloned.1.call-done = f32[2048,256]{1,0:T(8,128)} async-done(((f32[2048,256]{1,0:T(8,128)}), f32[2048,256]{1,0:T(8,128)}) %all-reduce.10.cloned.1.call-update) | async-done | bytes 2097168 | tf_op jit(solution)/shard_map/psum | solution.py:13
  688.6 64.6 %all-reduce.12.cloned.1.call-done = f32[2048,256]{1,0:T(8,128)} async-done(((f32[2048,256]{1,0:T(8,128)}), f32[2048,256]{1,0:T(8,128)}) %all-reduce.12.cloned.1.call-update) | async-done | bytes 2097168 | tf_op jit(solution)/shard_map/psum | solution.py:13
  753.1 10.5 convolution_subtract_fusion.1
  768.2 11.7 %cholesky.164 = f32[128,128]{1,0:T(8,128)S(1)} custom-call(f32[128,128]{1,0:T(8,128)S(1)} %cholesky.197), custom_call_target="Cholesky" | custom-call | tf_op jit(solution)/shard_map/jit(cholesky)/cholesky | solution.py:110
  780.0 9.8 custom-call.15
  790.2 11.7 %cholesky.181 = f32[128,128]{1,0:T(8,128)S(1)} custom-call(f32[128,128]{1,0:T(8,128)S(1)} %convolution_subtract_fusion.4), custom_call_target="Cholesky" | custom-call | tf_op jit(solution)/shard_map/jit(cholesky)/cholesky | solution.py:110
  808.9 19.9 %custom-call.16 = f32[2,128,128]{1,2,0:T(8,128)S(1)} custom-call(f32[2,128,128]{2,1,0:T(8,128)S(1)} %get-tuple-element.43), custom_call_target="InvertDiagBlocksLowerTriangular" | custom-call | tf_op jit(solution)/shard_map/triangular_solve/custom-call.0 | solution.py:111
  830.8 60.3 %all-reduce.14.cloned.1.call-done = f32[2,256,256]{2,1,0:T(8,128)} async-done(((f32[2,256,256]{2,1,0:T(8,128)}), f32[2,256,256]{2,1,0:T(8,128)}) %all-reduce.14.cloned.1.call-update) | async-done | bytes 524304 | tf_op jit(solution)/shard_map/psum | solution.py:13
  898.7 89.8 %all-reduce.16.cloned.1.call-done = f32[2048,256]{1,0:T(8,128)} async-done(((f32[2048,256]{1,0:T(8,128)}), f32[2048,256]{1,0:T(8,128)}) %all-reduce.16.cloned.1.call-update) | async-done | bytes 2097168 | tf_op jit(solution)/shard_map/psum | solution.py:13
  995.7 59.9 %all-reduce.18.cloned.1.call-done = f32[2048,256]{1,0:T(8,128)} async-done(((f32[2048,256]{1,0:T(8,128)}), f32[2048,256]{1,0:T(8,128)}) %all-reduce.18.cloned.1.call-update) | async-done | bytes 2097168 | tf_op jit(solution)/shard_map/psum | solution.py:13
  1055.6 11.9 %convolution_subtract_fusion = f32[2048,1024]{0,1:T(8,128)} fusion(f32[2048,1024]{0,1:T(8,128)} %copy-done.2, f32[2048,256]{1,0:T(8,128)} %all-reduce.16.cloned.1.call-done, f32[2048,256]{1,0:T(8,128)} %all-reduce.18.cloned.1.call-done, s32[]{:T(128)S(6)} %select_n.189), kind=kOutput, calls=%fused_computation.9 | convolution fusion | flops 6444548096 | bytes 19922948 | tf_op jit(solution)/shard_map/dot_general | solution.py:23
  (136 shorter events, 126.5 us)
Async XLA Ops:
  7.2 1.2 copy-start
  11.2 3.4 copy-start.4
  14.6 8.3 copy-start.5
  14.6 156.0 %all-to-all-start = ((f32[16,256,512]{2,1,0:T(8,128)}), f32[16,256,512]{2,1,0:T(8,128)}, u32[]{:S(2)}, u32[]{:S(2)}) async-start(f32[16,256,512]{2,1,0:T(8,128)} %bitcast.178), calls=%async_computation | async-start | bytes 16777216 | tf_op jit(solution)/shard_map/all_to_all | solution.py:55
  186.1 54.4 %all-to-all-start.1 = ((f32[8,2,256,256]{3,2,1,0:T(8,128)}), f32[8,2,256,256]{3,2,1,0:T(8,128)}, u32[]{:S(2)}, u32[]{:S(2)}) async-start(f32[8,2,256,256]{3,2,1,0:T(8,128)} %bitcast.176), calls=%async_computation.1 | async-start | bytes 8388608 | tf_op jit(solution)/shard_map/all_to_all | solution.py:67
  256.8 153.4 %all-to-all-start.2 = ((f32[16,2,256,256]{3,2,1,0:T(8,128)}), f32[16,2,256,256]{3,2,1,0:T(8,128)}, u32[]{:S(2)}, u32[]{:S(2)}) async-start(f32[16,2,256,256]{3,2,1,0:T(8,128)} %copy.34), calls=%async_computation.2 | async-start | bytes 16777216 | tf_op jit(solution)/shard_map/all_to_all | solution.py:80
  265.2 322.7 %all-reduce.8.cloned.1.call-start = ((), (), s32[]{:S(2)}) async-start(), calls=%async_computation.3 | async-start | bytes 1048576 | tf_op jit(solution)/shard_map/psum | solution.py:13
  524.8 160.5 %all-reduce.10.cloned.1.call-start = ((), (), s32[]{:S(2)}) async-start(), calls=%async_computation.4 | async-start | bytes 4194304 | tf_op jit(solution)/shard_map/psum | solution.py:13
  595.5 157.7 %all-reduce.12.cloned.1.call-start = ((), (), s32[]{:S(2)}) async-start(), calls=%async_computation.5 | async-start | bytes 4194304 | tf_op jit(solution)/shard_map/psum | solution.py:13
  685.3 67.9 %copy-start.3 = (f32[2048,256]{1,0:T(8,128)S(1)}, f32[2048,256]{1,0:T(8,128)}, u32[]{:S(2)}) copy-start(f32[2048,256]{1,0:T(8,128)} %all-reduce.10.cloned.1.call-done) | copy-start | bytes 6291460
  688.5 202.6 %all-reduce.14.cloned.1.call-start = ((), (), s32[]{:S(2)}) async-start(), calls=%async_computation.6 | async-start | bytes 1048576 | tf_op jit(solution)/shard_map/psum | solution.py:13
  763.6 3.4 copy-start.2
  830.7 157.7 %all-reduce.16.cloned.1.call-start = ((), (), s32[]{:S(2)}) async-start(), calls=%async_computation.7 | async-start | bytes 4194304 | tf_op jit(solution)/shard_map/psum | solution.py:13
  898.6 156.9 %all-reduce.18.cloned.1.call-start = ((), (), s32[]{:S(2)}) async-start(), calls=%async_computation.8 | async-start | bytes 4194304 | tf_op jit(solution)/shard_map/psum | solution.py:13
  1055.6 21.1 %copy-start.1 = (f32[1,512,512]{2,1,0:T(8,128)S(1)}, f32[1,512,512]{2,1,0:T(8,128)}, u32[]{:S(2)}) copy-start(f32[1,512,512]{2,1,0:T(8,128)} %param.13) | copy-start | bytes 3145732
Sparse Core Ops, SparseCore 0:
  524.9 62.9 all-reduce.7
  595.6 89.6 all-reduce.9
  688.6 64.4 all-reduce.11
  830.8 60.1 all-reduce.13
  898.8 89.6 all-reduce.15
  991.7 63.8 all-reduce.17
